TPU v7x, 32 devices: a whole 2x2x4 slice. The times are simulated.
32 devices in a mesh: rep: 4 (over z), shard: 8 (over y, x, core).
Axes of the slice: x: 2, y: 2, z: 4, core: 2. Of those that a mesh axis runs over, the one named last changes fastest.
Arguments:
- tokens: bfloat16 [4096, 2048], P(('rep', 'shard')), may hold values from -6 to 6
- attn_gain: float32 [2048], replicated, may hold values from 0.5 to 1.5
- query_weight: bfloat16 [2048, 2048], P('shard'), may hold values from -0.5 to 0.5
- key_weight: bfloat16 [2048, 512], P('shard'), may hold values from -0.5 to 0.5
- value_weight: bfloat16 [2048, 512], P('shard'), may hold values from -0.5 to 0.5
- output_weight: bfloat16 [2048, 2048], P('shard'), may hold values from -1 to 1
- ffn_gain: float32 [2048], replicated, may hold values from 0.5 to 1.5
- gate_weight: bfloat16 [2048, 8192], P('shard'), may hold values from -0.125 to 0.125
- up_weight: bfloat16 [2048, 8192], P('shard'), may hold values from -0.125 to 0.125
- down_weight: bfloat16 [8192, 2048], P('shard'), may hold values from -0.25 to 0.25
- dealing: int32 [4, 1024], P('rep'), may hold values from 0 to 1023, each once within a row
- lengths: int32 [4, 3], P('rep'), may hold values from 1 to 768, 1024 in all within a row
- cotangent: bfloat16 [4096, 2048], P(('rep', 'shard')), may hold values from -6 to 6
Outputs:
- layer_output: bfloat16 [4096, 2048], P(('rep', 'shard'))
- tokens_grad: float32 [4096, 2048], P(('rep', 'shard'))
- attn_gain_grad: float32 [2048], replicated
- query_weight_grad: float32 [2048, 2048], P('shard')
- key_weight_grad: float32 [2048, 512], P('shard')
- value_weight_grad: float32 [2048, 512], P('shard')
- output_weight_grad: float32 [2048, 2048], P('shard')
- ffn_gain_grad: float32 [2048], replicated
- gate_weight_grad: float32 [2048, 8192], P('shard')
- up_weight_grad: float32 [2048, 8192], P('shard')
- down_weight_grad: float32 [8192, 2048], P('shard')
Inputs may be any that keep to these rules, and one draw needn't show every extreme that they name: Each row of dealing is a permutation of 0 to 1023. Each row of lengths sums to 1024 and holds one length of exactly 768.
All inputs are finite; a program needn't handle non-finite values.
Results may differ from a plain program's by a relative error of at most 0.023.
Values may be sent and summed in bfloat16 or wider, within the bound.
A program may use at most 640 MiB of HBM per device.

v0:
```python
import jax
import jax.numpy as jnp
from jax import lax
from jax.sharding import PartitionSpec as P

HEADS = 32
KV_HEADS = 8
HEAD = 64
EPSILON = 1e-05
RESIDUAL_SCALE = 0.22
SCORE_SCALE = 0.015625
ROPE_BASE = 10000000.0
MASKED = -1e30


def rms_scale(hidden, gain_vector):
    return (
        hidden
        * lax.rsqrt(jnp.mean(hidden * hidden, axis=-1, keepdims=True) + EPSILON)
        * gain_vector
    )


def places(packed_index, seq_lengths):
    seq_ends = jnp.cumsum(seq_lengths)
    starts = seq_ends - seq_lengths
    segment = jnp.sum((packed_index[:, None] >= seq_ends[None, :]).astype(jnp.int32), axis=1)
    chosen = segment[:, None] == jnp.arange(seq_lengths.shape[0], dtype=jnp.int32)[None, :]
    position = packed_index - jnp.sum(jnp.where(chosen, starts[None, :], 0), axis=1)
    return (segment, position)


def angles(position, half_width):
    frequency = ROPE_BASE ** (
        -(jnp.arange(half_width, dtype=jnp.float32) * 2.0) / (2.0 * half_width)
    )
    turned = position.astype(jnp.float32)[:, None] * frequency[None, :]
    return (jnp.cos(turned)[:, None, :], jnp.sin(turned)[:, None, :])


def rotate(values, cosine, sine_table):
    half_width = values.shape[-1] // 2
    first_half = values[..., :half_width]
    second = values[..., half_width:]
    return jnp.concatenate(
        [first_half * cosine - second * sine_table, second * cosine + first_half * sine_table],
        axis=-1,
    )


def unrotate(values, cosine, sine_table):
    half_width = values.shape[-1] // 2
    first_half = values[..., :half_width]
    second = values[..., half_width:]
    return jnp.concatenate(
        [first_half * cosine + second * sine_table, second * cosine - first_half * sine_table],
        axis=-1,
    )


def picker(wanted, running, shard_piece):
    inside = (wanted >= 0) & (wanted < shard_piece.shape[0])
    picked = jnp.take(shard_piece, jnp.clip(wanted, 0, shard_piece.shape[0] - 1), axis=0)
    return running + jnp.where(inside[:, None], picked, jnp.zeros_like(picked))


def add_rows(inputs, shard_piece):
    return jnp.dot(inputs, shard_piece, preferred_element_type=jnp.float32)


def times_transposed(gradient, shard_piece):
    return lax.dot_general(
        gradient, shard_piece, (((1,), (1,)), ((), ())), preferred_element_type=jnp.float32
    )


def single_rows(inputs, weight):
    return add_rows(inputs, lax.all_gather(weight, "shard", axis=0, tiled=True))


def single_cols(gradient, weight):
    return times_transposed(gradient, lax.all_gather(weight, "shard", axis=0, tiled=True))


def spread(inputs, gradient):
    return lax.psum_scatter(
        lax.dot_general(
            inputs, gradient, (((0,), (0,)), ((), ())), preferred_element_type=jnp.float32
        ).astype(jnp.bfloat16),
        "shard",
        scatter_dimension=0,
        tiled=True,
    ).astype(jnp.float32)


def block_scores(queries, key_block, query_segment, query_position, key_segment, key_position):
    raw_scores = jnp.einsum(
        "rkgd,ckd->kgrc", queries, key_block, preferred_element_type=jnp.float32
    )
    allowed = (key_segment[None, :] == query_segment[:, None]) & (
        key_position[None, :] <= query_position[:, None]
    )
    return (SCORE_SCALE * raw_scores, allowed)


def per_device(
    tokens,
    attn_gain,
    query_weight,
    key_weight,
    value_weight,
    output_weight,
    ffn_gain,
    gate_weight,
    up_weight,
    down_weight,
    dealing,
    lengths,
    cotangent,
):
    local_rows = tokens.shape[0]
    model_width = tokens.shape[1]
    group_rows = local_rows * lax.axis_size("shard")
    kv_count = KV_HEADS
    head_width = HEAD
    per_group = HEADS // KV_HEADS
    here_index = lax.axis_index("shard")
    order_row = dealing[0]
    key_segment, key_position = places(order_row, lengths[0])
    query_segment = lax.dynamic_slice_in_dim(key_segment, here_index * local_rows, local_rows)
    query_position = lax.dynamic_slice_in_dim(key_position, here_index * local_rows, local_rows)
    my_tokens = lax.dynamic_slice_in_dim(order_row, here_index * local_rows, local_rows)
    cosine, sine_table = angles(query_position, head_width // 2)
    placed = picker(
        my_tokens,
        jnp.zeros((local_rows, model_width), jnp.bfloat16),
        lax.all_gather(tokens, "shard", axis=0, tiled=True),
    )
    hidden = placed.astype(jnp.float32)
    normed = rms_scale(hidden, attn_gain).astype(jnp.bfloat16)
    shard_pieces = (
        lax.all_gather(query_weight, "shard", axis=0, tiled=True),
        lax.all_gather(key_weight, "shard", axis=0, tiled=True),
        lax.all_gather(value_weight, "shard", axis=0, tiled=True),
    )
    query_pre = add_rows(normed, shard_pieces[0])
    key_pre = add_rows(normed, shard_pieces[1])
    value_pre = add_rows(normed, shard_pieces[2])
    queries = (
        rotate(query_pre.reshape(local_rows, HEADS, head_width), cosine, sine_table)
        .astype(jnp.bfloat16)
        .reshape(local_rows, kv_count, per_group, head_width)
    )
    key_local = (
        rotate(key_pre.reshape(local_rows, kv_count, head_width), cosine, sine_table)
        .astype(jnp.bfloat16)
        .reshape(local_rows, kv_count * head_width)
    )
    value_local = value_pre.astype(jnp.bfloat16)
    key_all, value_all = (
        lax.all_gather(key_local, "shard", axis=0, tiled=True),
        lax.all_gather(value_local, "shard", axis=0, tiled=True),
    )
    block_rows = 4 * local_rows
    block_count = group_rows // block_rows
    key_blocks = key_all.reshape(block_count, block_rows, kv_count, head_width)
    value_blocks = value_all.reshape(block_count, block_rows, kv_count, head_width)
    segment_blocks = key_segment.reshape(block_count, block_rows)
    position_blocks = key_position.reshape(block_count, block_rows)

    def gather_stats(running, block_item):
        running_top, running_sum = running
        key_block, segment_block, position_block = block_item
        scaled, allowed = block_scores(
            queries, key_block, query_segment, query_position, segment_block, position_block
        )
        masked_scores = jnp.where(allowed, scaled, MASKED)
        new_top = jnp.maximum(running_top, jnp.max(masked_scores, axis=-1))
        exponent = jnp.where(allowed, jnp.exp(masked_scores - new_top[..., None]), 0.0)
        running_sum = running_sum * jnp.exp(running_top - new_top) + jnp.sum(exponent, axis=-1)
        return ((new_top, running_sum), None)

    start_top = jnp.full((kv_count, per_group, local_rows), MASKED, jnp.float32)
    start_sum = jnp.zeros((kv_count, per_group, local_rows), jnp.float32)
    (score_top, score_sum), unused_stats = lax.scan(
        gather_stats, (start_top, start_sum), (key_blocks, segment_blocks, position_blocks)
    )
    log_total = score_top + jnp.log(score_sum)

    def weigh_values(running, block_item):
        upper_part, lower_part = running
        key_block, value_block, segment_block, position_block = block_item
        scaled, allowed = block_scores(
            queries, key_block, query_segment, query_position, segment_block, position_block
        )
        probabilities = jnp.where(allowed, jnp.exp(scaled - log_total[..., None]), 0.0)
        probs_high = probabilities.astype(jnp.bfloat16)
        probs_rest = (probabilities - probs_high.astype(jnp.float32)).astype(jnp.bfloat16)
        upper_part = upper_part + jnp.einsum(
            "kgrc,ckd->rkgd", probs_high, value_block, preferred_element_type=jnp.float32
        )
        lower_part = lower_part + jnp.einsum(
            "kgrc,ckd->rkgd", probs_rest, value_block, preferred_element_type=jnp.float32
        )
        return ((upper_part, lower_part), None)

    empty_heads = jnp.zeros((local_rows, kv_count, per_group, head_width), jnp.float32)
    (upper_part, lower_part), unused_weigh = lax.scan(
        weigh_values,
        (empty_heads, empty_heads),
        (key_blocks, value_blocks, segment_blocks, position_blocks),
    )
    attention = upper_part.astype(jnp.bfloat16).reshape(local_rows, model_width)
    attn_branch = single_rows(attention, output_weight)
    middle = hidden + RESIDUAL_SCALE * attn_branch
    normed_ffn = rms_scale(middle, ffn_gain).astype(jnp.bfloat16)
    shard_pieces = (
        lax.all_gather(gate_weight, "shard", axis=0, tiled=True),
        lax.all_gather(up_weight, "shard", axis=0, tiled=True),
    )
    gate_pre = add_rows(normed_ffn, shard_pieces[0])
    up_pre = add_rows(normed_ffn, shard_pieces[1])
    activated = (jax.nn.silu(gate_pre) * up_pre).astype(jnp.bfloat16)
    down_out = single_rows(activated, down_weight)
    layer_output = (middle + RESIDUAL_SCALE * down_out).astype(jnp.bfloat16)
    out_grad = cotangent.astype(jnp.float32)
    down_grad = (RESIDUAL_SCALE * out_grad).astype(jnp.bfloat16)
    down_weight_part = spread(activated, down_grad)
    act_grad = single_cols(down_grad, down_weight)
    unused_value, silu_pull = jax.vjp(
        lambda gate_in, up_in: jax.nn.silu(gate_in) * up_in, gate_pre, up_pre
    )
    gate_grad, up_grad = silu_pull(act_grad)
    gate_grad = gate_grad.astype(jnp.bfloat16)
    up_grad = up_grad.astype(jnp.bfloat16)
    gate_weight_part = spread(normed_ffn, gate_grad)
    up_weight_part = spread(normed_ffn, up_grad)
    shard_pieces = lax.all_gather((gate_weight, up_weight), "shard", axis=0, tiled=True)
    normed_ffn_grad = times_transposed(gate_grad, shard_pieces[0]) + times_transposed(
        up_grad, shard_pieces[1]
    )
    unused_norm, ffn_pull = jax.vjp(rms_scale, middle, ffn_gain)
    middle_part, ffn_gain_part = ffn_pull(normed_ffn_grad)
    middle_grad = out_grad + middle_part
    branch_grad = (RESIDUAL_SCALE * middle_grad).astype(jnp.bfloat16)
    output_weight_part = spread(attention, branch_grad)
    attention_grad = single_cols(branch_grad, output_weight)
    attention_grad = attention_grad.astype(jnp.bfloat16).reshape(
        local_rows, kv_count, per_group, head_width
    )
    row_delta = jnp.einsum(
        "rkgd,rkgd->kgr", attention_grad.astype(jnp.float32), upper_part + lower_part
    )

    def backward_block(query_grad, block_item):
        key_block, value_block, segment_block, position_block = block_item
        scaled, allowed = block_scores(
            queries, key_block, query_segment, query_position, segment_block, position_block
        )
        probabilities = jnp.where(allowed, jnp.exp(scaled - log_total[..., None]), 0.0)
        probs_grad = jnp.einsum(
            "rkgd,ckd->kgrc", attention_grad, value_block, preferred_element_type=jnp.float32
        )
        score_grad = (probabilities * (probs_grad - row_delta[..., None])).astype(jnp.bfloat16)
        query_grad = query_grad + SCORE_SCALE * jnp.einsum(
            "kgrc,ckd->rkgd", score_grad, key_block, preferred_element_type=jnp.float32
        )
        key_part = SCORE_SCALE * jnp.einsum(
            "kgrc,rkgd->ckd", score_grad, queries, preferred_element_type=jnp.float32
        )
        value_part = jnp.einsum(
            "kgrc,rkgd->ckd",
            probabilities.astype(jnp.bfloat16),
            attention_grad,
            preferred_element_type=jnp.float32,
        )
        return (query_grad, (key_part, value_part))

    query_grad, (key_parts, value_parts) = lax.scan(
        backward_block, empty_heads, (key_blocks, value_blocks, segment_blocks, position_blocks)
    )
    key_sum, value_sum = (
        lax.psum_scatter(
            key_parts.reshape(group_rows, kv_count * head_width).astype(jnp.bfloat16),
            "shard",
            scatter_dimension=0,
            tiled=True,
        ).astype(jnp.float32),
        lax.psum_scatter(
            value_parts.reshape(group_rows, kv_count * head_width).astype(jnp.bfloat16),
            "shard",
            scatter_dimension=0,
            tiled=True,
        ).astype(jnp.float32),
    )
    query_pre_grad = (
        unrotate(query_grad.reshape(local_rows, HEADS, head_width), cosine, sine_table)
        .reshape(local_rows, model_width)
        .astype(jnp.bfloat16)
    )
    key_pre_grad = (
        unrotate(key_sum.reshape(local_rows, kv_count, head_width), cosine, sine_table)
        .reshape(local_rows, kv_count * head_width)
        .astype(jnp.bfloat16)
    )
    value_pre_grad = value_sum.astype(jnp.bfloat16)
    query_weight_part = spread(normed, query_pre_grad)
    key_weight_part = spread(normed, key_pre_grad)
    value_weight_part = spread(normed, value_pre_grad)
    shard_pieces = lax.all_gather(
        (query_weight, key_weight, value_weight), "shard", axis=0, tiled=True
    )
    normed_grad = (
        times_transposed(query_pre_grad, shard_pieces[0])
        + times_transposed(key_pre_grad, shard_pieces[1])
        + times_transposed(value_pre_grad, shard_pieces[2])
    )
    unused_first, attn_pull = jax.vjp(rms_scale, hidden, attn_gain)
    hidden_part, attn_gain_part = attn_pull(normed_grad)
    dealt_grad = middle_grad + hidden_part
    inverse = (
        jnp.zeros((group_rows,), jnp.int32)
        .at[order_row]
        .set(jnp.arange(group_rows, dtype=jnp.int32))
    )
    wanted_slots = lax.dynamic_slice_in_dim(inverse, here_index * local_rows, local_rows)
    tokens_grad = picker(
        wanted_slots,
        jnp.zeros((local_rows, model_width), jnp.float32),
        lax.all_gather(dealt_grad.astype(jnp.bfloat16), "shard", axis=0, tiled=True).astype(
            jnp.float32
        ),
    )
    summed = (
        lax.psum(query_weight_part.astype(jnp.bfloat16), "rep").astype(jnp.float32),
        lax.psum(key_weight_part.astype(jnp.bfloat16), "rep").astype(jnp.float32),
        lax.psum(value_weight_part.astype(jnp.bfloat16), "rep").astype(jnp.float32),
        lax.psum(output_weight_part.astype(jnp.bfloat16), "rep").astype(jnp.float32),
        lax.psum(gate_weight_part.astype(jnp.bfloat16), "rep").astype(jnp.float32),
        lax.psum(up_weight_part.astype(jnp.bfloat16), "rep").astype(jnp.float32),
        lax.psum(down_weight_part.astype(jnp.bfloat16), "rep").astype(jnp.float32),
    )
    attn_gain_grad, ffn_gain_grad = lax.psum((attn_gain_part, ffn_gain_part), ("rep", "shard"))
    return (
        layer_output,
        tokens_grad,
        attn_gain_grad,
        summed[0],
        summed[1],
        summed[2],
        summed[3],
        ffn_gain_grad,
        summed[4],
        summed[5],
        summed[6],
    )


def solution(mesh):
    return jax.shard_map(
        per_device,
        mesh=mesh,
        in_specs=(
            P(("rep", "shard"), None),
            P(),
            P("shard", None),
            P("shard", None),
            P("shard", None),
            P("shard", None),
            P(),
            P("shard", None),
            P("shard", None),
            P("shard", None),
            P("rep", None),
            P("rep", None),
            P(("rep", "shard"), None),
        ),
        out_specs=(
            P(("rep", "shard"), None),
            P(("rep", "shard"), None),
            P(),
            P("shard", None),
            P("shard", None),
            P("shard", None),
            P("shard", None),
            P(),
            P("shard", None),
            P("shard", None),
            P("shard", None),
        ),
        check_vma=False,
    )
```

profile of v0, /device:TPU:0, one launch (start us, length us, event | category | flops | bytes accessed | tf_op | source)
XLA Modules:
  0.0 2409.0 jit_solution(6717161342337709093)
XLA Ops:
  11.5 37.9 %all-gather.12.cloned.1.call-done = bf16[1024,2048]{1,0:T(8,128)(2,1)} async-done(((bf16[128,2048]{1,0:T(8,128)(2,1)}), bf16[1024,2048]{1,0:T(8,128)(2,1)}) %all-gather.12.cloned.1.call-update) | async-done | bytes 4194320 | tf_op jit(solution)/shard_map/all_gather | solution.py:137
  53.9 25.3 %all-gather.14.cloned.1.call-done = bf16[2048,512]{1,0:T(8,128)(2,1)} async-done(((bf16[256,512]{1,0:T(8,128)(2,1)}), bf16[2048,512]{1,0:T(8,128)(2,1)}) %all-gather.14.cloned.1.call-update) | async-done | bytes 2097168 | tf_op jit(solution)/shard_map/all_gather | solution.py:144
  82.7 26.3 %all-gather.18.cloned.1.call-done = bf16[2048,512]{1,0:T(8,128)(2,1)} async-done(((bf16[256,512]{1,0:T(8,128)(2,1)}), bf16[2048,512]{1,0:T(8,128)(2,1)}) %all-gather.18.cloned.1.call-update) | async-done | bytes 2097168 | tf_op jit(solution)/shard_map/all_gather | solution.py:143
  142.1 18.7 all-gather.20.cloned.1.call-done
  164.8 52.1 %all-gather.22.cloned.1.call-done = bf16[2048,2048]{1,0:T(8,128)(2,1)} async-done(((bf16[256,2048]{1,0:T(8,128)(2,1)}), bf16[2048,2048]{1,0:T(8,128)(2,1)}) %all-gather.22.cloned.1.call-update) | async-done | bytes 8388624 | tf_op jit(solution)/shard_map/all_gather | solution.py:142
  224.1 19.2 while.41
  243.3 30.6 %while.42 = (s32[]{:T(128)}, f32[128,8,4,64]{0,3,2,1:T(8,128)S(1)}, f32[128,8,4,64]{0,3,2,1:T(8,128)}, bf16[2,512,8,64]{1,3,2,0:T(8,128)(2,1)}, s32[2,512]{1,0:T...) while((s32[]{:T(128)}, f32[128,8,4,64]{0,3,2,1:T(8,128)S(1)}, ...), condition=%wide.region_9.10_spmd.clone, body=%wide.region_8.9_spmd.clone.sunk | while | flops 829620224 | bytes 77837592 | solution.py:208
  281.3 154.7 %all-gather.26.cloned.1.call-done = bf16[2048,8192]{1,0:T(8,128)(2,1)} async-done(((bf16[256,8192]{1,0:T(8,128)(2,1)}), bf16[2048,8192]{1,0:T(8,128)(2,1)}) %all-gather.26.cloned.1.call-update) | async-done | bytes 33554448 | tf_op jit(solution)/shard_map/all_gather | solution.py:218
  436.0 19.2 fusion.109
  455.2 143.5 %all-gather.28.cloned.1.call-done = bf16[2048,8192]{1,0:T(8,128)(2,1)} async-done(((bf16[256,8192]{1,0:T(8,128)(2,1)}), bf16[2048,8192]{1,0:T(8,128)(2,1)}) %all-gather.28.cloned.1.call-update) | async-done | bytes 33554448 | tf_op jit(solution)/shard_map/all_gather | solution.py:219
  598.7 19.3 fusion.110
  618.0 143.3 %all-gather.30.cloned.1.call-done = bf16[8192,2048]{1,0:T(8,128)(2,1)} async-done(((bf16[1024,2048]{1,0:T(8,128)(2,1)}), bf16[8192,2048]{1,0:T(8,128)(2,1)}) %all-gather.30.cloned.1.call-update) | async-done | bytes 33554448 | tf_op jit(solution)/shard_map/all_gather | solution.py:78
  761.3 21.2 multiply_convert_fusion
  798.7 18.2 multiply_reduce_fusion
  831.0 40.0 %while.43 = (s32[]{:T(128)}, f32[128,8,4,64]{0,3,2,1:T(8,128)S(1)}, bf16[2,512,8,64]{1,3,2,0:T(8,128)(2,1)}, bf16[2,512,8,64]{1,3,2,0:T(8,128)(2,1)}, bf16[2,512...) while((s32[]{:T(128)}, f32[128,8,4,64]{0,3,2,1:T(8,128)S(1)}, ...), condition=%wide.region_14.15_spmd.clone, body=%wide.region_13.14_spmd.clone.sunk | while | flops 1364393984 | bytes 129758592 | solution.py:279
  886.2 28.5 %reduce-scatter.28.cloned.1.call-done = bf16[128,512]{1,0:T(8,128)(2,1)} async-done(((bf16[1024,512]{1,0:T(8,128)(2,1)}), bf16[128,512]{1,0:T(8,128)(2,1)}) %reduce-scatter.28.cloned.1.call-update) | async-done | bytes 131088
  918.2 36.2 %reduce-scatter.30.cloned.1.call-done = bf16[128,512]{1,0:T(8,128)(2,1)} async-done(((bf16[1024,512]{1,0:T(8,128)(2,1)}), bf16[128,512]{1,0:T(8,128)(2,1)}) %reduce-scatter.30.cloned.1.call-update) | async-done | bytes 131088
  1043.7 75.2 %reduce-scatter.14.cloned.1.call-done = bf16[256,2048]{1,0:T(8,128)(2,1)} async-done(((bf16[2048,2048]{1,0:T(8,128)(2,1)}), bf16[256,2048]{1,0:T(8,128)(2,1)}) %reduce-scatter.14.cloned.1.call-update) | async-done | bytes 1048592 | tf_op jit(solution)/shard_map/reduce_scatter | solution.py:86
  1118.9 75.6 %reduce-scatter.20.cloned.1.call-done = bf16[256,2048]{1,0:T(8,128)(2,1)} async-done(((bf16[2048,2048]{1,0:T(8,128)(2,1)}), bf16[256,2048]{1,0:T(8,128)(2,1)}) %reduce-scatter.20.cloned.1.call-update) | async-done | bytes 1048592 | tf_op jit(solution)/shard_map/reduce_scatter | solution.py:86
  1194.5 208.7 %reduce-scatter.22.cloned.1.call-done = bf16[256,8192]{1,0:T(8,128)(2,1)} async-done(((bf16[2048,8192]{1,0:T(8,128)(2,1)}), bf16[256,8192]{1,0:T(8,128)(2,1)}) %reduce-scatter.22.cloned.1.call-update) | async-done | bytes 4194320 | tf_op jit(solution)/shard_map/reduce_scatter | solution.py:86
  1403.2 209.1 %reduce-scatter.24.cloned.1.call-done = bf16[256,8192]{1,0:T(8,128)(2,1)} async-done(((bf16[2048,8192]{1,0:T(8,128)(2,1)}), bf16[256,8192]{1,0:T(8,128)(2,1)}) %reduce-scatter.24.cloned.1.call-update) | async-done | bytes 4194320 | tf_op jit(solution)/shard_map/reduce_scatter | solution.py:86
  1612.3 208.8 %reduce-scatter.26.cloned.1.call-done = bf16[1024,2048]{1,0:T(8,128)(2,1)} async-done(((bf16[8192,2048]{1,0:T(8,128)(2,1)}), bf16[1024,2048]{1,0:T(8,128)(2,1)}) %reduce-scatter.26.cloned.1.call-update) | async-done | bytes 4194320 | tf_op jit(solution)/shard_map/reduce_scatter | solution.py:86
  1840.0 39.9 %all-reduce = (f32[2048]{0:T(1024)}, f32[2048]{0:T(1024)}) all-reduce(f32[2048]{0:T(1024)S(1)} %get-tuple-element.438, f32[2048]{0:T(1024)S(1)} %copy-done.37), channel_id=1, replica_groups=mesh['rep'=4,'shard'=8] {'rep','shard'}, use_global_device_ids=true, to_apply=%region_19.20 | all-reduce | flops 4096 | bytes 32768 | tf_op jit(solution)/shard_map/psum | solution.py:343
  1892.6 486.6 %all-reduce.4.cloned.1.call-done = (bf16[256,2048]{1,0:T(8,128)(2,1)}, bf16[256,512]{1,0:T(8,128)(2,1)}, bf16[256,512]{1,0:T(8,128)(2,1)}, bf16[256,2048]{1,0:T(...) async-done(((bf16[256,2048]{1,0:T(8,128)(2,1)}, bf16[256,512]{1,0:T(8,128)(2,1)}, bf16[256,512]{1,0:T(8,128)(2,1)}, ...) | async-done | bytes 15204368 | tf_op jit(solution)/shard_map/psum | solution.py:335
  (282 shorter events, 344.4 us)
Async XLA Ops:
  7.2 42.2 %all-gather.12.cloned.1.call-start = ((), (), s32[]{:S(2)}) async-start(), calls=%async_computation.9 | async-start | bytes 4718592 | tf_op jit(solution)/shard_map/all_gather | solution.py:137
  7.9 71.3 %all-gather.14.cloned.1.call-start = ((), (), s32[]{:S(2)}) async-start(), calls=%async_computation.10 | async-start | bytes 2359296 | tf_op jit(solution)/shard_map/all_gather | solution.py:144
  8.7 100.4 %all-gather.18.cloned.1.call-start = ((), (), s32[]{:S(2)}) async-start(), calls=%async_computation.12 | async-start | bytes 2359296 | tf_op jit(solution)/shard_map/all_gather | solution.py:143
  9.4 125.5 %all-gather.16.cloned.1.call-start = ((), (), s32[]{:S(2)}) async-start(), calls=%async_computation.11 | async-start | bytes 1179648 | tf_op jit(solution)/shard_map/all_gather | solution.py:162
  82.0 78.8 %all-gather.20.cloned.1.call-start = ((), (), s32[]{:S(2)}) async-start(), calls=%async_computation.13 | async-start | bytes 1179648 | tf_op jit(solution)/shard_map/all_gather | solution.py:161
  112.4 104.6 %all-gather.22.cloned.1.call-start = ((), (), s32[]{:S(2)}) async-start(), calls=%async_computation.14 | async-start | bytes 9437184 | tf_op jit(solution)/shard_map/all_gather | solution.py:142
  113.0 162.0 %all-gather.24.cloned.1.call-start = ((), (), s32[]{:S(2)}) async-start(), calls=%async_computation.15 | async-start | bytes 9437184 | tf_op jit(solution)/shard_map/all_gather | solution.py:78
  113.7 322.2 %all-gather.26.cloned.1.call-start = ((), (), s32[]{:S(2)}) async-start(), calls=%async_computation.16 | async-start | bytes 37748736 | tf_op jit(solution)/shard_map/all_gather | solution.py:218
  114.5 484.2 %all-gather.28.cloned.1.call-start = ((), (), s32[]{:S(2)}) async-start(), calls=%async_computation.17 | async-start | bytes 37748736 | tf_op jit(solution)/shard_map/all_gather | solution.py:219
  115.2 646.0 %all-gather.30.cloned.1.call-start = ((), (), s32[]{:S(2)}) async-start(), calls=%async_computation.18 | async-start | bytes 37748736 | tf_op jit(solution)/shard_map/all_gather | solution.py:78
  115.8 799.0 %reduce-scatter.28.cloned.1.call-start = ((), (), s32[]{:S(2)}) async-start(), calls=%async_computation.27 | async-start | bytes 1179648
  878.6 75.8 %reduce-scatter.30.cloned.1.call-start = ((), (), s32[]{:S(2)}) async-start(), calls=%async_computation.28 | async-start | bytes 1179648
  886.2 142.0 %reduce-scatter.16.cloned.1.call-start = ((), (), s32[]{:S(2)}) async-start(), calls=%async_computation.21 | async-start | bytes 2359296 | tf_op jit(solution)/shard_map/reduce_scatter | solution.py:86
  918.1 125.5 %reduce-scatter.18.cloned.1.call-start = ((), (), s32[]{:S(2)}) async-start(), calls=%async_computation.22 | async-start | bytes 2359296 | tf_op jit(solution)/shard_map/reduce_scatter | solution.py:86
  957.6 161.2 %reduce-scatter.14.cloned.1.call-start = ((), (), s32[]{:S(2)}) async-start(), calls=%async_computation.20 | async-start | bytes 9437184 | tf_op jit(solution)/shard_map/reduce_scatter | solution.py:86
  964.0 230.5 %reduce-scatter.20.cloned.1.call-start = ((), (), s32[]{:S(2)}) async-start(), calls=%async_computation.23 | async-start | bytes 9437184 | tf_op jit(solution)/shard_map/reduce_scatter | solution.py:86
  969.8 433.3 %reduce-scatter.22.cloned.1.call-start = ((), (), s32[]{:S(2)}) async-start(), calls=%async_computation.24 | async-start | bytes 37748736 | tf_op jit(solution)/shard_map/reduce_scatter | solution.py:86
  985.6 626.7 %reduce-scatter.24.cloned.1.call-start = ((), (), s32[]{:S(2)}) async-start(), calls=%async_computation.25 | async-start | bytes 37748736 | tf_op jit(solution)/shard_map/reduce_scatter | solution.py:86
  1001.4 819.7 %reduce-scatter.26.cloned.1.call-start = ((), (), s32[]{:S(2)}) async-start(), calls=%async_computation.26 | async-start | bytes 37748736 | tf_op jit(solution)/shard_map/reduce_scatter | solution.py:86
  1018.2 861.7 %all-gather.32.cloned.1.call-start = ((), (), s32[]{:S(2)}) async-start(), calls=%async_computation.19 | async-start | bytes 4718592 | tf_op jit(solution)/shard_map/all_gather | solution.py:330
  1028.1 793.1 %copy-start.36 = (s32[1,1024]{1,0:T(1,128)S(1)}, s32[1,1024]{1,0:T(1,128)}, u32[]{:S(2)}) copy-start(s32[1,1024]{1,0:T(1,128)} %param.29) | copy-start | bytes 12292
  1028.1 797.5 %copy-start.5 = (f32[128,2048]{1,0:T(8,128)S(1)}, f32[128,2048]{1,0:T(8,128)}, u32[]{:S(2)}) copy-start(f32[128,2048]{1,0:T(8,128)} %copy-done.4) | copy-start | bytes 3145732
  1028.1 797.5 %copy-start.9 = (bf16[128,8192]{1,0:T(8,128)(2,1)S(1)}, bf16[128,8192]{1,0:T(8,128)(2,1)}, u32[]{:S(2)}) copy-start(bf16[128,8192]{1,0:T(8,128)(2,1)} %get-tuple-element.531) | copy-start | bytes 6291460
  1028.1 1351.1 %all-reduce.4.cloned.1.call-start = ((), (), s32[]{:S(2)}) async-start(), calls=%async_computation.29 | async-start | bytes 30408704 | tf_op jit(solution)/shard_map/psum | solution.py:335
  (51 other events, 1667.2 us)
Sparse Core Ops, SparseCore 0:
  9.9 39.4 all-gather.11
  51.3 27.8 all-gather.13
  81.1 27.9 all-gather.17
  111.4 23.4 all-gather.15
  137.2 23.5 all-gather.19
  162.5 54.3 all-gather.21
  218.8 54.4 all-gather.23
  275.2 160.7 all-gather.25
  437.9 160.7 all-gather.27
  600.4 160.7 all-gather.29
  878.7 36.0 reduce-scatter.27
  918.4 35.9 reduce-scatter.29
  957.7 41.1 reduce-scatter.15
  1002.4 41.2 reduce-scatter.17
  1047.5 71.2 reduce-scatter.13
  1123.1 71.2 reduce-scatter.19
  1197.9 205.2 reduce-scatter.21
  1407.0 205.2 reduce-scatter.23
  1615.9 205.2 reduce-scatter.25
  1823.6 37.2 all-gather.31
  1864.7 514.4 all-reduce.3
where the time goes:
time: 2410 us
  waiting for transfers between devices  1970 us (82%)
  matrix products  272 us (11%)
  local copies, waits for them, and re-layouts  57.5 us (2%)
  other arithmetic  53.1 us (2%)
  blocking collectives  39.9 us (2%)
    reduce_scatter x7, waiting for transfers between devices, spread(): lax.psum_scatter(lax.dot_general(inputs, gradient, (((0,), (0,)), ((), ()...  793 us
    psum x1, waiting for transfers between devices, per_device(): lax.psum(query_weight_part.astype(jnp.bfloat16), 'rep').astype(jnp.float32)  487 us
    all_gather x1, waiting for transfers between devices, per_device(): lax.all_gather(gate_weight, 'shard', axis=0, tiled=True)  155 us
    all_gather x1, waiting for transfers between devices, per_device(): lax.all_gather(up_weight, 'shard', axis=0, tiled=True)  144 us
    all_gather x2, waiting for transfers between devices, single_rows(): return add_rows(inputs, lax.all_gather(weight, 'shard', axis=0, tiled=True))  143 us
    dot_general x7, matrix products, times_transposed(): lax.dot_general(gradient, shard_piece, (((1,), (1,)), ((), ())), preferre...  71.1 us
    unnamed x23, waiting for transfers between devices  70.2 us
    dot_general x7, matrix products, add_rows(): return jnp.dot(inputs, shard_piece, preferred_element_type=jnp.float32)  70.2 us
  transfers between devices with their start and end apart: 21, of which 18 were waited for; matrix products, arithmetic and copies ran while one was open for 10% of the time, Pallas kernels for 0%

commit v1 on v0

--- a/solution.py
+++ b/solution.py
@@ -11,6 +11,11 @@
 SCORE_SCALE = 0.015625
 ROPE_BASE = 10000000.0
 MASKED = -1e30
+
+
+def summed_here(x, mesh_axis):
+    shards = lax.all_gather(x, mesh_axis)
+    return jnp.sum(shards, axis=0)
 
 
 def rms_scale(hidden, gain_vector):
@@ -332,7 +337,7 @@
         ),
     )
     summed = (
-        lax.psum(query_weight_part.astype(jnp.bfloat16), "rep").astype(jnp.float32),
+        summed_here(query_weight_part.astype(jnp.bfloat16), "rep").astype(jnp.float32),
         lax.psum(key_weight_part.astype(jnp.bfloat16), "rep").astype(jnp.float32),
         lax.psum(value_weight_part.astype(jnp.bfloat16), "rep").astype(jnp.float32),
         lax.psum(output_weight_part.astype(jnp.bfloat16), "rep").astype(jnp.float32),

time: 2410 us -> 2460 us (1.021)
  waiting for transfers between devices: 1970 us -> 2010 us
    all_gather x0 -> x1, waiting for transfers between devices: none -> 50.5 us  [summed_here(): shards = lax.all_gather(x, mesh_axis)]
    unnamed x23 -> x24, waiting for transfers between devices: 70.2 us -> 63.8 us
  transfers between devices with their start and end apart: 21 -> 22, of which waited for: 18 -> 20; matrix products, arithmetic and copies ran while one was open for 10% -> 10% of each run, Pallas kernels for 0% -> 0%
where the time goes in v1:
time: 2460 us; the launch traced here: 2450 us
  waiting for transfers between devices  2010 us (82%)
  matrix products  274 us (11%)
  local copies, waits for them, and re-layouts  57.6 us (2%)
  other arithmetic  57 us (2%)
  blocking collectives  39.9 us (2%)
    reduce_scatter x7, waiting for transfers between devices, spread(): lax.psum_scatter(lax.dot_general(inputs, gradient, (((0,), (0,)), ((), ()...  797 us
    psum x1, waiting for transfers between devices, per_device(): lax.psum(key_weight_part.astype(jnp.bfloat16), 'rep').astype(jnp.float32)  478 us
    all_gather x1, waiting for transfers between devices, per_device(): lax.all_gather(gate_weight, 'shard', axis=0, tiled=True)  155 us
    all_gather x1, waiting for transfers between devices, per_device(): lax.all_gather(up_weight, 'shard', axis=0, tiled=True)  144 us
    all_gather x2, waiting for transfers between devices, single_rows(): return add_rows(inputs, lax.all_gather(weight, 'shard', axis=0, tiled=True))  143 us
    dot_general x7, matrix products, times_transposed(): lax.dot_general(gradient, shard_piece, (((1,), (1,)), ((), ())), preferre...  72 us
    dot_general x7, matrix products, add_rows(): return jnp.dot(inputs, shard_piece, preferred_element_type=jnp.float32)  70.2 us
    dot_general x7, matrix products, spread(): lax.dot_general(inputs, gradient, (((0,), (0,)), ((), ())), preferred_ele...  66 us
  transfers between devices with their start and end apart: 22, of which 20 were waited for; matrix products, arithmetic and copies ran while one was open for 10% of the time, Pallas kernels for 0%

profile of v1, /device:TPU:0, one launch (start us, length us, event | category | flops | bytes accessed | tf_op | source)
XLA Modules:
  0.0 2454.8 jit_solution(6213050016543146827)
XLA Ops:
  11.5 37.9 %all-gather.14.cloned.1.call-done = bf16[1024,2048]{1,0:T(8,128)(2,1)} async-done(((bf16[128,2048]{1,0:T(8,128)(2,1)}), bf16[1024,2048]{1,0:T(8,128)(2,1)}) %all-gather.14.cloned.1.call-update) | async-done | bytes 4194320 | tf_op jit(solution)/shard_map/all_gather | solution.py:142
  53.9 25.3 %all-gather.16.cloned.1.call-done = bf16[2048,512]{1,0:T(8,128)(2,1)} async-done(((bf16[256,512]{1,0:T(8,128)(2,1)}), bf16[2048,512]{1,0:T(8,128)(2,1)}) %all-gather.16.cloned.1.call-update) | async-done | bytes 2097168 | tf_op jit(solution)/shard_map/all_gather | solution.py:149
  82.7 26.3 %all-gather.20.cloned.1.call-done = bf16[2048,512]{1,0:T(8,128)(2,1)} async-done(((bf16[256,512]{1,0:T(8,128)(2,1)}), bf16[2048,512]{1,0:T(8,128)(2,1)}) %all-gather.20.cloned.1.call-update) | async-done | bytes 2097168 | tf_op jit(solution)/shard_map/all_gather | solution.py:148
  164.8 52.1 %all-gather.24.cloned.1.call-done = bf16[2048,2048]{1,0:T(8,128)(2,1)} async-done(((bf16[256,2048]{1,0:T(8,128)(2,1)}), bf16[2048,2048]{1,0:T(8,128)(2,1)}) %all-gather.24.cloned.1.call-update) | async-done | bytes 8388624 | tf_op jit(solution)/shard_map/all_gather | solution.py:147
  224.1 19.2 while.41
  243.3 30.6 %while.42 = (s32[]{:T(128)}, f32[128,8,4,64]{0,3,2,1:T(8,128)S(1)}, f32[128,8,4,64]{0,3,2,1:T(8,128)}, bf16[2,512,8,64]{1,3,2,0:T(8,128)(2,1)}, s32[2,512]{1,0:T...) while((s32[]{:T(128)}, f32[128,8,4,64]{0,3,2,1:T(8,128)S(1)}, ...), condition=%wide.region_9.10_spmd.clone, body=%wide.region_8.9_spmd.clone.sunk | while | flops 829620224 | bytes 77837592 | solution.py:213
  281.3 154.6 %all-gather.28.cloned.1.call-done = bf16[2048,8192]{1,0:T(8,128)(2,1)} async-done(((bf16[256,8192]{1,0:T(8,128)(2,1)}), bf16[2048,8192]{1,0:T(8,128)(2,1)}) %all-gather.28.cloned.1.call-update) | async-done | bytes 33554448 | tf_op jit(solution)/shard_map/all_gather | solution.py:223
  436.0 19.2 fusion.109
  455.2 143.5 %all-gather.30.cloned.1.call-done = bf16[2048,8192]{1,0:T(8,128)(2,1)} async-done(((bf16[256,8192]{1,0:T(8,128)(2,1)}), bf16[2048,8192]{1,0:T(8,128)(2,1)}) %all-gather.30.cloned.1.call-update) | async-done | bytes 33554448 | tf_op jit(solution)/shard_map/all_gather | solution.py:224
  598.7 19.3 fusion.110
  618.0 143.3 %all-gather.32.cloned.1.call-done = bf16[8192,2048]{1,0:T(8,128)(2,1)} async-done(((bf16[1024,2048]{1,0:T(8,128)(2,1)}), bf16[8192,2048]{1,0:T(8,128)(2,1)}) %all-gather.32.cloned.1.call-update) | async-done | bytes 33554448 | tf_op jit(solution)/shard_map/all_gather | solution.py:83
  761.3 21.4 multiply_convert_fusion
  831.3 39.7 %while.43 = (s32[]{:T(128)}, f32[128,8,4,64]{0,3,2,1:T(8,128)S(1)}, bf16[2,512,8,64]{1,3,2,0:T(8,128)(2,1)}, bf16[2,512,8,64]{1,3,2,0:T(8,128)(2,1)}, bf16[2,512...) while((s32[]{:T(128)}, f32[128,8,4,64]{0,3,2,1:T(8,128)S(1)}, ...), condition=%wide.region_14.15_spmd.clone, body=%wide.region_13.14_spmd.clone.sunk | while | flops 1364393984 | bytes 129758592 | solution.py:284
  892.7 22.1 reduce-scatter.28.cloned.1.call-done
  918.2 36.3 %reduce-scatter.30.cloned.1.call-done = bf16[128,512]{1,0:T(8,128)(2,1)} async-done(((bf16[1024,512]{1,0:T(8,128)(2,1)}), bf16[128,512]{1,0:T(8,128)(2,1)}) %reduce-scatter.30.cloned.1.call-update) | async-done | bytes 131088
  1029.8 44.7 %reduce-scatter.16.cloned.1.call-done = bf16[256,512]{1,0:T(8,128)(2,1)} async-done(((bf16[2048,512]{1,0:T(8,128)(2,1)}), bf16[256,512]{1,0:T(8,128)(2,1)}) %reduce-scatter.16.cloned.1.call-update) | async-done | bytes 262160 | tf_op jit(solution)/shard_map/reduce_scatter | solution.py:91
  1074.5 44.3 %reduce-scatter.18.cloned.1.call-done = bf16[256,512]{1,0:T(8,128)(2,1)} async-done(((bf16[2048,512]{1,0:T(8,128)(2,1)}), bf16[256,512]{1,0:T(8,128)(2,1)}) %reduce-scatter.18.cloned.1.call-update) | async-done | bytes 262160 | tf_op jit(solution)/shard_map/reduce_scatter | solution.py:91
  1118.9 75.6 %reduce-scatter.20.cloned.1.call-done = bf16[256,2048]{1,0:T(8,128)(2,1)} async-done(((bf16[2048,2048]{1,0:T(8,128)(2,1)}), bf16[256,2048]{1,0:T(8,128)(2,1)}) %reduce-scatter.20.cloned.1.call-update) | async-done | bytes 1048592 | tf_op jit(solution)/shard_map/reduce_scatter | solution.py:91
  1194.5 208.7 %reduce-scatter.22.cloned.1.call-done = bf16[256,8192]{1,0:T(8,128)(2,1)} async-done(((bf16[2048,8192]{1,0:T(8,128)(2,1)}), bf16[256,8192]{1,0:T(8,128)(2,1)}) %reduce-scatter.22.cloned.1.call-update) | async-done | bytes 4194320 | tf_op jit(solution)/shard_map/reduce_scatter | solution.py:91
  1403.2 209.1 %reduce-scatter.24.cloned.1.call-done = bf16[256,8192]{1,0:T(8,128)(2,1)} async-done(((bf16[2048,8192]{1,0:T(8,128)(2,1)}), bf16[256,8192]{1,0:T(8,128)(2,1)}) %reduce-scatter.24.cloned.1.call-update) | async-done | bytes 4194320 | tf_op jit(solution)/shard_map/reduce_scatter | solution.py:91
  1612.3 208.8 %reduce-scatter.26.cloned.1.call-done = bf16[1024,2048]{1,0:T(8,128)(2,1)} async-done(((bf16[8192,2048]{1,0:T(8,128)(2,1)}), bf16[1024,2048]{1,0:T(8,128)(2,1)}) %reduce-scatter.26.cloned.1.call-update) | async-done | bytes 4194320 | tf_op jit(solution)/shard_map/reduce_scatter | solution.py:91
  1840.0 39.9 %all-reduce = (f32[2048]{0:T(1024)}, f32[2048]{0:T(1024)}) all-reduce(f32[2048]{0:T(1024)S(1)} %get-tuple-element.438, f32[2048]{0:T(1024)S(1)} %copy-done.36), channel_id=1, replica_groups=mesh['rep'=4,'shard'=8] {'rep','shard'}, use_global_device_ids=true, to_apply=%region_19.20 | all-reduce | flops 4096 | bytes 32768 | tf_op jit(solution)/shard_map/psum | solution.py:348
  1892.7 50.5 %all-gather.36.cloned.1.call-done = bf16[1024,2048]{1,0:T(8,128)(2,1)} async-done(((bf16[256,2048]{1,0:T(8,128)(2,1)}), bf16[1024,2048]{1,0:T(8,128)(2,1)}) %all-gather.36.cloned.1.call-update) | async-done | bytes 4194320 | tf_op jit(solution)/shard_map/all_gather | solution.py:17
  1947.8 477.7 %all-reduce.4.cloned.1.call-done = (bf16[256,512]{1,0:T(8,128)(2,1)}, bf16[256,512]{1,0:T(8,128)(2,1)}, bf16[256,2048]{1,0:T(8,128)(2,1)}, bf16[256,8192]{1,0:T(...) async-done(((bf16[256,512]{1,0:T(8,128)(2,1)}, bf16[256,512]{1,0:T(8,128)(2,1)}, bf16[256,2048]{1,0:T(8,128)(2,1)}, bf16[256,8192]{1,0:T(8,128)(2,1)}, ...) | async-done | bytes 14155792 | tf_op jit(solution)/shard_map/psum | solution.py:341
  (284 shorter events, 377.8 us)
Async XLA Ops:
  7.2 42.2 %all-gather.14.cloned.1.call-start = ((), (), s32[]{:S(2)}) async-start(), calls=%async_computation.9 | async-start | bytes 4718592 | tf_op jit(solution)/shard_map/all_gather | solution.py:142
  7.9 71.3 %all-gather.16.cloned.1.call-start = ((), (), s32[]{:S(2)}) async-start(), calls=%async_computation.10 | async-start | bytes 2359296 | tf_op jit(solution)/shard_map/all_gather | solution.py:149
  8.7 100.4 %all-gather.20.cloned.1.call-start = ((), (), s32[]{:S(2)}) async-start(), calls=%async_computation.12 | async-start | bytes 2359296 | tf_op jit(solution)/shard_map/all_gather | solution.py:148
  9.4 125.5 %all-gather.18.cloned.1.call-start = ((), (), s32[]{:S(2)}) async-start(), calls=%async_computation.11 | async-start | bytes 1179648 | tf_op jit(solution)/shard_map/all_gather | solution.py:167
  82.0 78.8 %all-gather.22.cloned.1.call-start = ((), (), s32[]{:S(2)}) async-start(), calls=%async_computation.13 | async-start | bytes 1179648 | tf_op jit(solution)/shard_map/all_gather | solution.py:166
  112.4 104.6 %all-gather.24.cloned.1.call-start = ((), (), s32[]{:S(2)}) async-start(), calls=%async_computation.14 | async-start | bytes 9437184 | tf_op jit(solution)/shard_map/all_gather | solution.py:147
  113.0 161.9 %all-gather.26.cloned.1.call-start = ((), (), s32[]{:S(2)}) async-start(), calls=%async_computation.15 | async-start | bytes 9437184 | tf_op jit(solution)/shard_map/all_gather | solution.py:83
  113.7 322.2 %all-gather.28.cloned.1.call-start = ((), (), s32[]{:S(2)}) async-start(), calls=%async_computation.16 | async-start | bytes 37748736 | tf_op jit(solution)/shard_map/all_gather | solution.py:223
  114.5 484.2 %all-gather.30.cloned.1.call-start = ((), (), s32[]{:S(2)}) async-start(), calls=%async_computation.17 | async-start | bytes 37748736 | tf_op jit(solution)/shard_map/all_gather | solution.py:224
  115.2 646.0 %all-gather.32.cloned.1.call-start = ((), (), s32[]{:S(2)}) async-start(), calls=%async_computation.18 | async-start | bytes 37748736 | tf_op jit(solution)/shard_map/all_gather | solution.py:83
  115.8 799.0 %reduce-scatter.28.cloned.1.call-start = ((), (), s32[]{:S(2)}) async-start(), calls=%async_computation.28 | async-start | bytes 1179648
  878.6 75.8 %reduce-scatter.30.cloned.1.call-start = ((), (), s32[]{:S(2)}) async-start(), calls=%async_computation.29 | async-start | bytes 1179648
  886.2 143.6 %reduce-scatter.14.cloned.1.call-start = ((), (), s32[]{:S(2)}) async-start(), calls=%async_computation.20 | async-start | bytes 9437184 | tf_op jit(solution)/shard_map/reduce_scatter | solution.py:91
  892.4 182.1 %reduce-scatter.16.cloned.1.call-start = ((), (), s32[]{:S(2)}) async-start(), calls=%async_computation.21 | async-start | bytes 2359296 | tf_op jit(solution)/shard_map/reduce_scatter | solution.py:91
  918.1 200.7 %reduce-scatter.18.cloned.1.call-start = ((), (), s32[]{:S(2)}) async-start(), calls=%async_computation.22 | async-start | bytes 2359296 | tf_op jit(solution)/shard_map/reduce_scatter | solution.py:91
  957.7 236.8 %reduce-scatter.20.cloned.1.call-start = ((), (), s32[]{:S(2)}) async-start(), calls=%async_computation.23 | async-start | bytes 9437184 | tf_op jit(solution)/shard_map/reduce_scatter | solution.py:91
  963.5 439.7 %reduce-scatter.22.cloned.1.call-start = ((), (), s32[]{:S(2)}) async-start(), calls=%async_computation.24 | async-start | bytes 37748736 | tf_op jit(solution)/shard_map/reduce_scatter | solution.py:91
  981.0 631.2 %reduce-scatter.24.cloned.1.call-start = ((), (), s32[]{:S(2)}) async-start(), calls=%async_computation.25 | async-start | bytes 37748736 | tf_op jit(solution)/shard_map/reduce_scatter | solution.py:91
  996.9 824.2 %reduce-scatter.26.cloned.1.call-start = ((), (), s32[]{:S(2)}) async-start(), calls=%async_computation.26 | async-start | bytes 37748736 | tf_op jit(solution)/shard_map/reduce_scatter | solution.py:91
  1013.7 866.3 %all-gather.34.cloned.1.call-start = ((), (), s32[]{:S(2)}) async-start(), calls=%async_computation.19 | async-start | bytes 4718592 | tf_op jit(solution)/shard_map/all_gather | solution.py:335
  1024.3 801.4 %copy-start.5 = (f32[128,2048]{1,0:T(8,128)S(1)}, f32[128,2048]{1,0:T(8,128)}, u32[]{:S(2)}) copy-start(f32[128,2048]{1,0:T(8,128)} %copy-done.4) | copy-start | bytes 3145732
  1024.3 801.4 %copy-start.9 = (bf16[128,8192]{1,0:T(8,128)(2,1)S(1)}, bf16[128,8192]{1,0:T(8,128)(2,1)}, u32[]{:S(2)}) copy-start(bf16[128,8192]{1,0:T(8,128)(2,1)} %get-tuple-element.530) | copy-start | bytes 6291460
  1024.3 918.9 %all-gather.36.cloned.1.call-start = ((), (), s32[]{:S(2)}) async-start(), calls=%async_computation.27 | async-start | bytes 5242880 | tf_op jit(solution)/shard_map/all_gather | solution.py:17
  1029.8 1395.7 %all-reduce.4.cloned.1.call-start = ((), (), s32[]{:S(2)}) async-start(), calls=%async_computation.30 | async-start | bytes 28311552 | tf_op jit(solution)/shard_map/psum | solution.py:341
  (51 other events, 2460.1 us)
Sparse Core Ops, SparseCore 0:
  9.9 39.4 all-gather.13
  51.3 27.8 all-gather.15
  81.1 27.9 all-gather.19
  111.4 23.4 all-gather.17
  137.2 23.5 all-gather.21
  162.5 54.3 all-gather.23
  218.8 54.4 all-gather.25
  275.2 160.7 all-gather.27
  437.9 160.7 all-gather.29
  600.4 160.7 all-gather.31
  878.7 36.0 reduce-scatter.27
  918.4 35.9 reduce-scatter.29
  958.5 71.2 reduce-scatter.13
  1033.3 41.2 reduce-scatter.15
  1077.6 41.1 reduce-scatter.17
  1123.1 71.2 reduce-scatter.19
  1197.9 205.2 reduce-scatter.21
  1407.0 205.2 reduce-scatter.23
  1615.9 205.2 reduce-scatter.25
  1823.6 37.2 all-gather.33
  1862.5 80.5 all-gather.35
  1946.8 478.6 all-reduce.3
